TPU v7x, 256 devices: a whole 4x4x8 slice. The times are simulated.
256 devices in a mesh: ctx: 16 (over y, x), exp: 8 (over z), dp: 2 (over core).
Axes of the slice: x: 4, y: 4, z: 8, core: 2. Of those that a mesh axis runs over, the one named last changes fastest.
Arguments:
- residual: bfloat16 [2048, 4096], P('ctx', ('exp', 'dp')), may hold values from -6 to 6
- ssm_values: bfloat16 [2048, 4096], P('ctx', ('exp', 'dp')), may hold values from -6 to 6
- ssm_keys: bfloat16 [2048, 64], P('ctx'), may hold values from -6 to 6
- ssm_queries: bfloat16 [2048, 64], P('ctx'), may hold values from -0.015625 to 0.015625
- log_decay: float32 [2048, 64], P('ctx', ('exp', 'dp')), may hold values from -1 to 0, as said below
- expert_ids: int32 [2048, 2], P('ctx'), may hold values from 0 to 7, all different within a row; in each aligned block of 128 rows (0 to 127, 128 to 255, ...) at most 40 rows name the same one
- gate_probs: float32 [2048, 2], P('ctx'), may hold values from 0.2 to 1
- norm_gain: float32 [4096], P(('exp', 'dp')), may hold values from 0.5 to 1.5
- w_gate: bfloat16 [8, 4096, 8192], P('exp', None, ('ctx', 'dp')), may hold values from -0.09375 to 0.09375
- w_up: bfloat16 [8, 4096, 8192], P('exp', None, ('ctx', 'dp')), may hold values from -0.09375 to 0.09375
- w_down: bfloat16 [8, 4096, 8192], P('exp', None, ('ctx', 'dp')), may hold values from -0.0625 to 0.0625
- out_grad: bfloat16 [2048, 4096], P('ctx', ('exp', 'dp')), may hold values from -6 to 6
Outputs:
- grad_residual: bfloat16 [2048, 4096], P('ctx', ('exp', 'dp'))
- grad_values: bfloat16 [2048, 4096], P('ctx', ('exp', 'dp'))
- grad_keys: float32 [2048, 64], P('ctx')
- grad_queries: float32 [2048, 64], P('ctx')
- grad_decay: float32 [2048, 64], P('ctx', ('exp', 'dp'))
- grad_probs: float32 [2048, 2], P('ctx')
- grad_gain: float32 [4096], P(('exp', 'dp'))
- w_gate_grad: bfloat16 [8, 4096, 8192], P('exp', None, ('ctx', 'dp'))
- w_up_grad: bfloat16 [8, 4096, 8192], P('exp', None, ('ctx', 'dp'))
- w_down_grad: bfloat16 [8, 4096, 8192], P('exp', None, ('ctx', 'dp'))
Inputs may be any that keep to these rules, and one draw needn't show every extreme that they name: `expert_ids`: each token names two different experts; among the 128 tokens of one index of ctx (aligned blocks) no expert is named more than 40 times, a bound that some block reaches. `log_decay`: negative everywhere.
All inputs are finite; a program needn't handle non-finite values.
Results may differ from a plain program's by a relative error of at most 0.028.
Values may be sent and summed in bfloat16 or wider, within the bound.
No kernel may reach another device: no remote copies, remote signals or barrier semaphores. Data moves between devices by JAX's collectives and lax.ppermute only.
A program may use at most 128 MiB of HBM per device.

v0:
```python
import jax
import jax.numpy as jnp
from jax import lax
from jax.sharding import PartitionSpec as P

HIGH = lax.Precision.HIGHEST
EPS = 1e-05


def entering(x, axis, join, neutral):
    place = lax.axis_index(axis)
    gathered = jax.tree.map(
        lambda a, kind: lax.all_gather(a.astype(kind), axis), x, (jnp.bfloat16, jnp.bfloat16)
    )
    state = jax.tree.map(lambda a, e: jnp.zeros_like(a) + jnp.asarray(e, a.dtype), x, neutral)

    def entering_one(step, state):
        return join(
            state,
            jax.tree.map(
                lambda a, own: lax.dynamic_index_in_dim(a, step, 0, False).astype(own.dtype),
                gathered,
                x,
            ),
        )

    return lax.fori_loop(0, place, entering_one, state)


def carried_in(x, axis, join, neutral):
    count = lax.axis_size(axis)
    place = lax.axis_index(axis)
    ahead = count - 1 - place
    gathered = jax.tree.map(
        lambda a, kind: lax.all_gather(a.astype(kind), axis),
        x,
        jax.tree.map(lambda a: jnp.bfloat16 if a.dtype == jnp.float32 else a.dtype, x),
    )
    state = jax.tree.map(lambda a, e: jnp.zeros_like(a) + jnp.asarray(e, a.dtype), x, neutral)

    def carried_one(step, state):
        source = count - 1 - step
        return join(
            state,
            jax.tree.map(
                lambda a, own: lax.dynamic_index_in_dim(a, source, 0, False).astype(own.dtype),
                gathered,
                x,
            ),
        )

    return lax.fori_loop(0, ahead, carried_one, state)


def block_state(values, key_rows, log_decay):
    cumulative = jnp.cumsum(log_decay, axis=0)
    total_log = cumulative[-1]
    tail_decay = jnp.exp(total_log[None, :] - cumulative)
    weighted = tail_decay[:, :, None] * values
    state_local = jnp.einsum("shp,sn->hpn", weighted, key_rows, precision=HIGH)
    return (jnp.exp(total_log), state_local)


def block_output(values, key_rows, queries, log_decay, state_in):
    cumulative = jnp.cumsum(log_decay, axis=0)
    length = values.shape[0]
    row_index = lax.broadcasted_iota(jnp.int32, (length, length), 0)
    col_index = lax.broadcasted_iota(jnp.int32, (length, length), 1)
    causal = (row_index >= col_index)[None]
    cum_heads = cumulative.T
    log_gap = jnp.where(causal, cum_heads[:, :, None] - cum_heads[:, None, :], 0.0)
    decay_mat = jnp.where(causal, jnp.exp(log_gap), 0.0)
    scores = jnp.dot(queries, key_rows.T, precision=HIGH)
    inner_part = jnp.einsum("hts,shp->thp", decay_mat * scores[None], values, precision=HIGH)
    carried = jnp.einsum("tn,hpn->thp", queries, state_in, precision=HIGH)
    return inner_part + jnp.exp(cumulative)[:, :, None] * carried


def silu_parts(gate_act):
    sigmoid_val = jax.nn.sigmoid(gate_act)
    return (gate_act * sigmoid_val, sigmoid_val * (1.0 + gate_act * (1.0 - sigmoid_val)))


def route_slots(token_ids, expert_count):
    owners = token_ids.reshape(-1)
    onehot = (owners[:, None] == jnp.arange(expert_count, dtype=jnp.int32)[None, :]).astype(
        jnp.int32
    )
    rank_before = jnp.cumsum(onehot, axis=0) - onehot
    return (owners, jnp.sum(rank_before * onehot, axis=1))


def combine_states(earlier_part, later_part):
    return (
        earlier_part[0] * later_part[0],
        later_part[0][:, None, None] * earlier_part[1] + later_part[1],
    )


def arrange_rows(gathered, ctx_count, dp_count):
    capacity = gathered.shape[1]
    exp_count = gathered.shape[2]
    feat = gathered.shape[3]
    shaped = gathered.reshape(ctx_count, dp_count, capacity, exp_count, feat)
    return shaped.transpose(0, 2, 3, 1, 4).reshape(
        ctx_count * capacity, exp_count * dp_count * feat
    )


def arrange_sums(full_term, ctx_count, dp_count, exp_count, capacity):
    feat = full_term.shape[1] // (exp_count * dp_count)
    shaped = full_term.reshape(ctx_count, capacity, exp_count, dp_count, feat)
    return shaped.transpose(0, 3, 1, 2, 4).reshape(
        ctx_count * dp_count * capacity, exp_count * feat
    )


def per_device(
    residual,
    ssm_values,
    ssm_keys,
    ssm_queries,
    log_decay,
    expert_ids,
    gate_probs,
    norm_gain,
    w_gate,
    w_up,
    w_down,
    out_grad,
):
    tokens = residual.shape[0]
    feat = residual.shape[1]
    heads_here = log_decay.shape[1]
    head_size = feat // heads_here
    model_width = w_gate.shape[1]
    ctx_count = lax.axis_size("ctx")
    exp_count = lax.axis_size("exp")
    dp_count = lax.axis_size("dp")
    expert_count = w_gate.shape[0] * exp_count
    capacity = 5 * tokens // (2 * expert_count)
    block_vals = ssm_values.astype(jnp.float32).reshape(tokens, heads_here, head_size)
    block_keys = ssm_keys.astype(jnp.float32)
    block_queries = ssm_queries.astype(jnp.float32)
    (decay_total, state_local), state_pull = jax.vjp(block_state, block_vals, block_keys, log_decay)
    neutral = (jnp.ones_like(decay_total), jnp.zeros_like(state_local))
    state_in = entering((decay_total, state_local), "ctx", combine_states, neutral)[1]
    mixer_out, output_pull = jax.vjp(
        block_output, block_vals, block_keys, block_queries, log_decay, state_in
    )
    hidden = (residual.astype(jnp.float32) + mixer_out.reshape(tokens, feat)).astype(jnp.bfloat16)
    hidden_f = hidden.astype(jnp.float32)
    square_sum = lax.psum(jnp.sum(hidden_f * hidden_f, axis=1), ("exp", "dp"))
    inv_rms = lax.rsqrt(square_sum / model_width + EPS)[:, None]
    normed = (hidden_f * inv_rms * norm_gain[None, :]).astype(jnp.bfloat16)
    owners, slot_index = route_slots(expert_ids, expert_count)
    pair_rows = jnp.repeat(normed, 2, axis=0)
    dout_rows = jnp.repeat(out_grad, 2, axis=0)
    pair_prob = gate_probs.reshape(-1)
    pair_cot = (pair_prob[:, None] * dout_rows.astype(jnp.float32)).astype(jnp.bfloat16)
    empty = jnp.zeros((expert_count, capacity, feat), jnp.bfloat16)
    send_rows = empty.at[owners, slot_index].set(pair_rows).reshape(expert_count, capacity, 1, feat)
    got_rows = lax.all_to_all(send_rows, "exp", split_axis=0, concat_axis=2, tiled=True)
    all_rows = lax.all_gather(got_rows, ("ctx", "dp"), axis=0, tiled=True)
    rows_flat = arrange_rows(all_rows, ctx_count, dp_count)
    act_gate = jnp.dot(rows_flat, w_gate[0], preferred_element_type=jnp.float32)
    act_up = jnp.dot(rows_flat, w_up[0], preferred_element_type=jnp.float32)
    swish_val, swish_slope = silu_parts(act_gate)
    hidden_act = (swish_val * act_up).astype(jnp.bfloat16)
    full_out = lax.dot_general(
        hidden_act, w_down[0], (((1,), (1,)), ((), ())), preferred_element_type=jnp.float32
    )
    out_total = lax.psum_scatter(
        arrange_sums(full_out, ctx_count, dp_count, exp_count, capacity).astype(jnp.bfloat16),
        ("ctx", "dp"),
        scatter_dimension=0,
        tiled=True,
    )
    expert_out = out_total.reshape(1, capacity, exp_count, feat)
    back_out = lax.all_to_all(expert_out, "exp", split_axis=2, concat_axis=0, tiled=True).reshape(
        expert_count, capacity, feat
    )
    out_pairs = back_out[owners, slot_index]
    probs_part = jnp.einsum(
        "kd,kd->k", out_pairs, dout_rows, preferred_element_type=jnp.float32
    ).reshape(tokens, 2)
    grad_probs = lax.psum(probs_part, ("exp", "dp"))
    send_cot = empty.at[owners, slot_index].set(pair_cot).reshape(expert_count, capacity, 1, feat)
    got_cot = lax.all_to_all(send_cot, "exp", split_axis=0, concat_axis=2, tiled=True)
    all_cot = lax.all_gather(got_cot, ("ctx", "dp"), axis=0, tiled=True)
    cot_flat = arrange_rows(all_cot, ctx_count, dp_count)
    grad_act = jnp.dot(cot_flat, w_down[0], preferred_element_type=jnp.float32)
    grad_gate = (grad_act * act_up * swish_slope).astype(jnp.bfloat16)
    grad_up = (grad_act * swish_val).astype(jnp.bfloat16)
    full_back = lax.dot_general(
        grad_gate, w_gate[0], (((1,), (1,)), ((), ())), preferred_element_type=jnp.float32
    ) + lax.dot_general(
        grad_up, w_up[0], (((1,), (1,)), ((), ())), preferred_element_type=jnp.float32
    )
    back_total = lax.psum_scatter(
        arrange_sums(full_back, ctx_count, dp_count, exp_count, capacity).astype(jnp.bfloat16),
        ("ctx", "dp"),
        scatter_dimension=0,
        tiled=True,
    )
    pair_back = back_total.reshape(1, capacity, exp_count, feat)
    back_in = lax.all_to_all(pair_back, "exp", split_axis=2, concat_axis=0, tiled=True).reshape(
        expert_count, capacity, feat
    )
    grad_normed = (
        back_in[owners, slot_index].astype(jnp.float32).reshape(tokens, 2, feat).sum(axis=1)
    )
    w_gate_grad = jnp.dot(rows_flat.T, grad_gate, preferred_element_type=jnp.float32).astype(
        jnp.bfloat16
    )[None]
    w_up_grad = jnp.dot(rows_flat.T, grad_up, preferred_element_type=jnp.float32).astype(
        jnp.bfloat16
    )[None]
    w_down_grad = jnp.dot(cot_flat.T, hidden_act, preferred_element_type=jnp.float32).astype(
        jnp.bfloat16
    )[None]
    scaled = grad_normed * norm_gain[None, :]
    inner_sum = lax.psum(jnp.sum(hidden_f * scaled, axis=1), ("exp", "dp"))
    projection = (inner_sum / model_width)[:, None]
    grad_hidden = (
        out_grad.astype(jnp.float32) + inv_rms * scaled - hidden_f * inv_rms**3 * projection
    )
    gain_part = jnp.sum(grad_normed * hidden_f * inv_rms, axis=0)
    grad_gain = lax.psum(gain_part, "ctx")
    grad_mixer = grad_hidden.reshape(tokens, heads_here, head_size)
    vals_first, keys_first, queries_part, decay_first, carry_cot = output_pull(grad_mixer)
    grad_state = carried_in((decay_total, carry_cot), "ctx", combine_states, neutral)[1]
    grad_total = jnp.sum(grad_state * state_in, axis=(1, 2))
    vals_second, keys_second, decay_second = state_pull((grad_total, grad_state))
    grad_keys, grad_queries = (
        lax.psum((keys_first + keys_second).astype(jnp.bfloat16), ("exp", "dp")).astype(
            jnp.float32
        ),
        lax.psum(queries_part.astype(jnp.bfloat16), ("exp", "dp")).astype(jnp.float32),
    )
    grad_residual = grad_hidden.astype(jnp.bfloat16)
    grad_values = (vals_first + vals_second).reshape(tokens, feat).astype(jnp.bfloat16)
    grad_decay = decay_first + decay_second
    return (
        grad_residual,
        grad_values,
        grad_keys,
        grad_queries,
        grad_decay,
        grad_probs,
        grad_gain,
        w_gate_grad,
        w_up_grad,
        w_down_grad,
    )


def solution(mesh):
    return jax.shard_map(
        per_device,
        mesh=mesh,
        in_specs=(
            P("ctx", ("exp", "dp")),
            P("ctx", ("exp", "dp")),
            P("ctx", None),
            P("ctx", None),
            P("ctx", ("exp", "dp")),
            P("ctx", None),
            P("ctx", None),
            P(("exp", "dp")),
            P("exp", None, ("ctx", "dp")),
            P("exp", None, ("ctx", "dp")),
            P("exp", None, ("ctx", "dp")),
            P("ctx", ("exp", "dp")),
        ),
        out_specs=(
            P("ctx", ("exp", "dp")),
            P("ctx", ("exp", "dp")),
            P("ctx", None),
            P("ctx", None),
            P("ctx", ("exp", "dp")),
            P("ctx", None),
            P(("exp", "dp")),
            P("exp", None, ("ctx", "dp")),
            P("exp", None, ("ctx", "dp")),
            P("exp", None, ("ctx", "dp")),
        ),
        check_vma=False,
    )
```

profile of v0, /device:TPU:2, one launch (start us, length us, event | category | flops | bytes accessed | tf_op | source)
XLA Modules:
  0.0 650.5 jit_solution(5369685150378966095)
XLA Ops:
  7.3 0.9 copy.158
  9.5 0.8 copy.161
  10.4 0.9 broadcast_in_dim.74
  11.6 13.2 %scatter_fusion = bf16[8,40,256]{2,1,0:T(8,128)(2,1)S(1)} fusion(bf16[8,40,256]{2,1,0:T(8,128)(2,1)S(1)} %broadcast_in_dim.73.clone.1, s32[256]{0:T(256)S(1)} %bitcast.193, bf16[256,256]{1,0:T(8,128)(2,1)S(1)} %fusion.19), kind=kCustom, calls=%fused_computation.2 | custom fusion | bytes 395264 | tf_op jit(solution)/shard_map/scatter | solution.py:188
  24.9 18.0 %all_to_all.66 = bf16[8,40,1,256]{3,1,2,0:T(8,128)(2,1)S(1)} all-to-all(bf16[8,40,1,256]{3,1,2,0:T(8,128)(2,1)S(1)} %bitcast.200), channel_id=1, replica_groups=mesh['ctx'=16,'exp'=8,'dp'=2] {'exp'}, dimensions={0} | all-to-all | bytes 327680 | tf_op jit(solution)/shard_map/all_to_all | solution.py:189
  44.6 20.7 %all-gather.4 = bf16[16,1,4]{2,1,0:T(2,128)(2,1)S(1)} all-gather(bf16[1,1,4]{2,1,0:T(2,128)(2,1)S(1)} %get-tuple-element.299), channel_id=1, replica_groups=mesh['ctx'=16,'exp'=8,'dp'=2] {'ctx'}, dimensions={0}, use_global_device_ids=true | all-gather | bytes 136 | tf_op jit(solution)/shard_map/all_gather | solution.py:13
  65.4 1.0 copy.152
  67.0 27.6 %all-gather = bf16[64,64,64]{2,1,0:T(8,128)(2,1)} all-gather(bf16[4,64,64]{2,1,0:T(8,128)(2,1)S(1)} %convolution_convert_fusion.4), channel_id=2, replica_groups=mesh['ctx'=16,'exp'=8,'dp'=2] {'ctx'}, dimensions={0}, use_global_device_ids=true | all-gather | bytes 557056 | tf_op jit(solution)/shard_map/all_gather | solution.py:13
  94.8 1.0 while.26
  94.9 0.9 convert_add_fusion.4
  96.7 23.5 %psum.42 = f32[128]{0:T(128)S(1)} all-reduce(f32[128]{0:T(128)S(1)} %get-tuple-element.291), channel_id=1, replica_groups=mesh['ctx'=16,'exp'=8,'dp'=2] {'exp','dp'}, use_global_device_ids=true, to_apply=%region_4.5 | all-reduce | flops 128 | bytes 1024 | tf_op jit(solution)/shard_map/psum | solution.py:153
  121.1 13.2 %scatter_fusion.1 = bf16[8,40,256]{2,1,0:T(8,128)(2,1)S(1)} fusion(bf16[8,40,256]{2,1,0:T(8,128)(2,1)S(1)} %broadcast_in_dim.73.clone, s32[256]{0:T(256)S(1)} %bitcast.194, bf16[256,256]{1,0:T(8,128)(2,1)S(1)} %reshape.273), kind=kCustom, calls=%fused_computation.3 | custom fusion | bytes 395264 | tf_op jit(solution)/shard_map/scatter | solution.py:162
  134.3 12.5 %all_to_all.67 = bf16[8,40,1,256]{3,1,2,0:T(8,128)(2,1)S(1)} all-to-all(bf16[8,40,1,256]{3,1,2,0:T(8,128)(2,1)S(1)} %bitcast.199), channel_id=1, replica_groups=mesh['ctx'=16,'exp'=8,'dp'=2] {'exp'}, dimensions={0} | all-to-all | bytes 327680 | tf_op jit(solution)/shard_map/all_to_all | solution.py:163
  148.1 13.0 %copy.164 = bf16[16,40,8,2,256]{4,3,2,1,0:T(2,128)(2,1)} copy(bf16[16,40,8,2,256]{4,2,1,3,0:T(8,128)(2,1)} %bitcast.203) | data formatting | bytes 10485760 | tf_op jit(solution)/shard_map/transpose | solution.py:105
  161.1 9.6 %reshape.236 = bf16[640,4096]{1,0:T(8,128)(2,1)} reshape(bf16[16,40,8,2,256]{4,3,2,1,0:T(2,128)(2,1)} %copy.164) | data formatting | bytes 10485760 | tf_op jit(solution)/shard_map/reshape | solution.py:105
  170.7 35.8 %all-gather.10.cloned.1.call-done = bf16[32,40,8,1,256]{4,2,3,1,0:T(8,128)(2,1)} async-done(((bf16[1,40,8,1,256]{4,2,3,1,0:T(8,128)(2,1)}), bf16[32,40,8,1,256]{4,2,3,1,0:T(8,128)(2,1)}) %all-gather.10.cloned.1.call-update) | async-done | bytes 5242896 | tf_op jit(solution)/shard_map/all_gather | solution.py:164
  206.6 13.0 %copy.167 = bf16[16,40,8,2,256]{4,3,2,1,0:T(2,128)(2,1)} copy(bf16[16,40,8,2,256]{4,2,1,3,0:T(8,128)(2,1)} %bitcast.204) | data formatting | bytes 10485760 | tf_op jit(solution)/shard_map/transpose | solution.py:105
  219.6 9.6 %reshape.240 = bf16[640,4096]{1,0:T(8,128)(2,1)} reshape(bf16[16,40,8,2,256]{4,3,2,1,0:T(2,128)(2,1)} %copy.167) | data formatting | bytes 10485760 | tf_op jit(solution)/shard_map/reshape | solution.py:105
  229.2 4.2 fusion.10
  233.9 1.5 fusion.5
  235.5 2.4 multiply_convert_fusion
  238.0 1.6 convert_bitcast_fusion
  239.6 2.3 copy.176
  241.9 4.6 copy.191
  247.0 1.1 copy-done.4
  248.2 1.6 fusion.3
  249.8 3.8 add_convert_fusion
  253.6 9.6 %convert_element_type.165 = bf16[16,40,8,2,256]{4,3,2,1,0:T(2,128)(2,1)} reshape(bf16[640,4096]{1,0:T(8,128)(2,1)} %add_convert_fusion) | data formatting | bytes 10485760 | tf_op jit(solution)/shard_map/convert_element_type | solution.py:201
  263.2 3.6 copy.168
  266.8 4.5 copy.189
  271.3 1.0 copy-done.10
  272.3 5.9 fusion.2
  278.2 60.3 %reduce-scatter.5.cloned.1.call-done = bf16[40,2048]{1,0:T(8,128)(2,1)} async-done(((bf16[1280,2048]{1,0:T(8,128)(2,1)}), bf16[40,2048]{1,0:T(8,128)(2,1)}) %reduce-scatter.5.cloned.1.call-update) | async-done | bytes 163856 | tf_op jit(solution)/shard_map/reduce_scatter | solution.py:173
  338.5 0.9 copy.192
  340.1 7.0 %all-to-all-start.3 = ((bf16[1,40,8,256]{3,1,0,2:T(8,128)(2,1)}), bf16[1,40,8,256]{3,1,0,2:T(8,128)(2,1)S(1)}, u32[]{:S(2)}, u32[]{:S(2)}) async-start(bf16[1,40,8,256]{3,1,0,2:T(8,128)(2,1)} %copy.177), calls=%async_computation.5 | async-start | bytes 327680 | tf_op jit(solution)/shard_map/all_to_all | solution.py:180
  347.2 5.7 fusion
  352.9 81.2 %reduce-scatter.3.cloned.1.call-done = bf16[40,2048]{1,0:T(8,128)(2,1)} async-done(((bf16[1280,2048]{1,0:T(8,128)(2,1)}), bf16[40,2048]{1,0:T(8,128)(2,1)}) %reduce-scatter.3.cloned.1.call-update) | async-done | bytes 163856 | tf_op jit(solution)/shard_map/reduce_scatter | solution.py:200
  434.1 0.9 copy.190
  435.8 7.2 %all-to-all-start.2 = ((bf16[1,40,8,256]{3,1,0,2:T(8,128)(2,1)}), bf16[1,40,8,256]{3,1,0,2:T(8,128)(2,1)S(1)}, u32[]{:S(2)}, u32[]{:S(2)}) async-start(bf16[1,40,8,256]{3,1,0,2:T(8,128)(2,1)} %copy.169), calls=%async_computation.3 | async-start | bytes 327680 | tf_op jit(solution)/shard_map/all_to_all | solution.py:207
  443.0 5.7 fusion.1
  448.7 1.7 gather_fusion.1
  450.6 1.7 all-to-all-done.2
  452.4 1.7 gather_fusion
  454.6 46.5 %all-reduce.1 = (f32[128]{0:T(128)S(1)}, f32[128,2]{1,0:T(8,128)S(1)}) all-reduce(f32[128]{0:T(128)S(1)} %get-tuple-element.264, f32[128,2]{1,0:T(8,128)S(1)} %reshape.247), channel_id=1, replica_groups=mesh['ctx'=16,'exp'=8,'dp'=2] {'exp','dp'}, use_global_device_ids=true, to_apply=%region_13.14 | all-reduce | flops 384 | bytes 3072 | tf_op jit(solution)/shard_map/psum | solution.py:223
  502.6 25.1 %all-gather.3 = bf16[64,64,64]{2,1,0:T(8,128)(2,1)} all-gather(bf16[4,64,64]{2,1,0:T(8,128)(2,1)S(1)} %convolution_convert_fusion.3), channel_id=5, replica_groups=mesh['ctx'=16,'exp'=8,'dp'=2] {'ctx'}, dimensions={0}, use_global_device_ids=true | all-gather | bytes 557056 | tf_op jit(solution)/shard_map/all_gather | solution.py:35
  527.7 22.9 %while.27 = (s32[]{:T(128)}, f32[4,64,64]{2,1,0:T(8,128)S(1)}, s32[]{:T(128)}, bf16[16,4]{1,0:T(8,128)(2,1)}, bf16[16,4,64,64]{3,2,1,0:T(8,128)(2,1)}, /*index=5*/s32[]{:T(128)}, s32[]{:T(128)}, s32[]{:T(128)}, s32[]{:T(128)}) while((s32[]{:T(128)}, f32[4,64,64]{2,1,0:T(8,128)S(1)}, s32[]{:T(128)}, bf16[16,4]{1,0:T(8,128)(2,1)}, ...), condition=%wide.region_15.16_spmd, body=%wide.region_14.15_spmd.sunk | while | flops 49162 | bytes 164035 | solution.py:52
  528.4 0.9 convert_add_fusion.5
  530.0 0.9 convert_add_fusion.5
  531.7 0.9 convert_add_fusion.5
  533.3 0.9 convert_add_fusion.5
  534.9 0.9 convert_add_fusion.5
  536.6 0.9 convert_add_fusion.5
  538.2 0.9 convert_add_fusion.5
  539.8 0.9 convert_add_fusion.5
  541.5 0.9 convert_add_fusion.5
  543.1 0.9 convert_add_fusion.5
  544.8 0.9 convert_add_fusion.5
  546.4 0.9 convert_add_fusion.5
  548.0 0.9 convert_add_fusion.5
  549.7 0.9 convert_add_fusion.5
  550.9 39.5 %psum.47 = f32[256]{0:T(256)} all-reduce(f32[256]{0:T(256)S(1)} %get-tuple-element.263), channel_id=1, replica_groups=mesh['ctx'=16,'exp'=8,'dp'=2] {'ctx'}, use_global_device_ids=true, to_apply=%region_30.31 | all-reduce | flops 256 | bytes 2048 | tf_op jit(solution)/shard_map/psum | solution.py:229
  593.7 45.7 %all-reduce.2 = (bf16[128,64]{0,1:T(8,128)(2,1)S(1)}, bf16[128,64]{0,1:T(8,128)(2,1)S(1)}) all-reduce(bf16[128,64]{0,1:T(8,128)(2,1)S(1)} %fusion.16, bf16[128,64]{0,1:T(8,128)(2,1)S(1)} %fusion.17), channel_id=1, replica_groups=mesh['ctx'=16,'exp'=8,'dp'=2] {'exp','dp'}, use_global_device_ids=true, to_apply=%region_17.18 | all-reduce | flops 16384 | bytes 65536 | tf_op jit(solution)/shard_map/psum | solution.py:236
  640.8 1.1 reduce_window_sum.47
  641.9 1.1 reduce_window_sum.48
  (139 shorter events, 27.4 us)
Async XLA Ops:
  7.2 222.0 %copy-start = (bf16[1,4096,256]{2,1,0:T(8,128)(2,1)S(1)}, bf16[1,4096,256]{2,1,0:T(8,128)(2,1)}, u32[]{:S(2)}) copy-start(bf16[1,4096,256]{2,1,0:T(8,128)(2,1)} %param.26) | copy-start | bytes 6291460
  7.2 59.6 %copy-start.13 = (bf16[128,64]{0,1:T(8,128)(2,1)S(1)}, bf16[128,64]{0,1:T(8,128)(2,1)}, u32[]{:S(2)}) copy-start(bf16[128,64]{0,1:T(8,128)(2,1)} %param.18) | copy-start | bytes 49156
  7.2 87.4 %copy-start.12 = (bf16[128,64]{0,1:T(8,128)(2,1)S(1)}, bf16[128,64]{0,1:T(8,128)(2,1)}, u32[]{:S(2)}) copy-start(bf16[128,64]{0,1:T(8,128)(2,1)} %param.19) | copy-start | bytes 49156
  7.2 89.4 %copy-start.16 = (bf16[128,256]{1,0:T(8,128)(2,1)S(1)}, bf16[128,256]{1,0:T(8,128)(2,1)}, u32[]{:S(2)}) copy-start(bf16[128,256]{1,0:T(8,128)(2,1)} %param.16) | copy-start | bytes 196612
  7.2 113.6 %copy-start.17 = (f32[256]{0:T(256)S(1)}, f32[256]{0:T(256)}, u32[]{:S(2)}) copy-start(f32[256]{0:T(256)} %param.23) | copy-start | bytes 3076
  7.2 140.9 %all-gather.8.cloned.1.call-start = ((), (), s32[]{:S(2)}) async-start(), calls=%async_computation.8 | async-start | bytes 5406720 | tf_op jit(solution)/shard_map/all_gather | solution.py:190
  43.6 163.0 %all-gather.10.cloned.1.call-start = ((), (), s32[]{:S(2)}) async-start(), calls=%async_computation.9 | async-start | bytes 5406720 | tf_op jit(solution)/shard_map/all_gather | solution.py:164
  66.4 67.9 %copy-start.19 = (f32[4,128]{1,0:T(4,128)}, f32[4,128]{1,0:T(4,128)S(1)}, u32[]{:S(2)}) copy-start(f32[4,128]{1,0:T(4,128)S(1)} %copy.150) | copy-start | bytes 6148
  94.8 39.5 %copy-start.14 = (f32[128,128]{1,0:T(8,128)}, f32[128,128]{1,0:T(8,128)S(1)}, u32[]{:S(2)}) copy-start(f32[128,128]{1,0:T(8,128)S(1)} %fusion.65) | copy-start | bytes 196612
  95.8 38.5 %copy-start.18 = (bf16[16,4]{1,0:T(8,128)(2,1)}, bf16[16,4]{1,0:T(8,128)(2,1)S(1)}, u32[]{:S(2)}) copy-start(bf16[16,4]{1,0:T(8,128)(2,1)S(1)} %get-tuple-element.437) | copy-start | bytes 388
  147.5 191.0 %reduce-scatter.5.cloned.1.call-start = ((), (), s32[]{:S(2)}) async-start(), calls=%async_computation.7 | async-start | bytes 5406720 | tf_op jit(solution)/shard_map/reduce_scatter | solution.py:173
  229.2 4.2 copy-start.2
  229.2 4.7 copy-start.3
  233.9 1.6 copy-start.5
  238.0 3.9 copy-start.9
  246.6 1.6 copy-start.4
  246.6 187.5 %reduce-scatter.3.cloned.1.call-start = ((), (), s32[]{:S(2)}) async-start(), calls=%async_computation.6 | async-start | bytes 5406720 | tf_op jit(solution)/shard_map/reduce_scatter | solution.py:200
  248.2 1.6 copy-start.6
  248.2 1.6 copy-start.7
  271.3 1.0 copy-start.10
  340.1 95.7 %all-to-all-start.3 = ((bf16[1,40,8,256]{3,1,0,2:T(8,128)(2,1)}), bf16[1,40,8,256]{3,1,0,2:T(8,128)(2,1)S(1)}, u32[]{:S(2)}, u32[]{:S(2)}) async-start(bf16[1,40,8,256]{3,1,0,2:T(8,128)(2,1)} %copy.177), calls=%async_computation.5 | async-start | bytes 327680 | tf_op jit(solution)/shard_map/all_to_all | solution.py:180
  347.2 95.8 %copy-start.8 = (bf16[640,256]{1,0:T(8,128)(2,1)S(1)}, bf16[640,256]{1,0:T(8,128)(2,1)}, u32[]{:S(2)}) copy-start(bf16[640,256]{1,0:T(8,128)(2,1)} %get-tuple-element.297) | copy-start | bytes 983044
  435.8 16.6 %all-to-all-start.2 = ((bf16[1,40,8,256]{3,1,0,2:T(8,128)(2,1)}), bf16[1,40,8,256]{3,1,0,2:T(8,128)(2,1)S(1)}, u32[]{:S(2)}, u32[]{:S(2)}) async-start(bf16[1,40,8,256]{3,1,0,2:T(8,128)(2,1)} %copy.169), calls=%async_computation.3 | async-start | bytes 327680 | tf_op jit(solution)/shard_map/all_to_all | solution.py:207
  443.0 58.1 %copy-start.11 = (bf16[128,256]{1,0:T(8,128)(2,1)S(1)}, bf16[128,256]{1,0:T(8,128)(2,1)}, u32[]{:S(2)}) copy-start(bf16[128,256]{1,0:T(8,128)(2,1)} %param.27) | copy-start | bytes 196612
  443.0 58.1 %copy-start.21 = (f32[128]{0:T(128)S(1)}, f32[128]{0:T(128)}, u32[]{:S(2)}) copy-start(f32[128]{0:T(128)} %get-tuple-element.300) | copy-start | bytes 1540
  448.7 142.3 %copy-start.15 = (f32[128,128]{1,0:T(8,128)S(1)}, f32[128,128]{1,0:T(8,128)}, u32[]{:S(2)}) copy-start(f32[128,128]{1,0:T(8,128)} %copy-done.14) | copy-start | bytes 196612
  448.7 142.3 %copy-start.20 = (f32[4,128]{1,0:T(4,128)S(1)}, f32[4,128]{1,0:T(4,128)}, u32[]{:S(2)}) copy-start(f32[4,128]{1,0:T(4,128)} %copy-done.19) | copy-start | bytes 6148
  452.4 191.4 %copy-start.1 = (bf16[1,4096,256]{2,1,0:T(8,128)(2,1)S(1)}, bf16[1,4096,256]{2,1,0:T(8,128)(2,1)}, u32[]{:S(2)}) copy-start(bf16[1,4096,256]{2,1,0:T(8,128)(2,1)} %param.26) | copy-start | bytes 6291460
Sparse Core Ops, SparseCore 0:
  43.7 49.1 all-gather.7
  147.6 58.8 all-gather.9
  246.7 91.7 reduce-scatter.4
  342.4 91.7 reduce-scatter.2
where the time goes:
time: 657 us; the launch traced here: 650 us
  blocking collectives  259 us (39%)
  waiting for transfers between devices  179 us (27%)
  local copies, waits for them, and re-layouts  116 us (18%)
  matrix products  35.9 us (5%)
  other arithmetic  30.4 us (5%)
  starting transfers between devices  15.3 us (2%)
  between operations  14.5 us (2%)
    reduce_scatter x1, waiting for transfers between devices, per_device(): lax.psum_scatter(arrange_sums(full_back, ctx_count, dp_count, exp_count,...  81.2 us
    reduce_scatter x1, waiting for transfers between devices, per_device(): lax.psum_scatter(arrange_sums(full_out, ctx_count, dp_count, exp_count, c...  60.3 us
    all_gather x2, blocking collectives, entering(): lax.all_gather(a.astype(kind), axis)  48.3 us
    psum x1, blocking collectives, per_device(): inner_sum = lax.psum(jnp.sum(hidden_f * scaled, axis=1), ('exp', 'dp'))  46.5 us
    psum x1, blocking collectives, per_device(): lax.psum((keys_first + keys_second).astype(jnp.bfloat16), ('exp', 'dp'))  45.7 us
    psum x1, blocking collectives, per_device(): grad_gain = lax.psum(gain_part, 'ctx')  39.5 us
    all_gather x1, waiting for transfers between devices, per_device(): all_rows = lax.all_gather(got_rows, ('ctx', 'dp'), axis=0, tiled=True)  35.8 us
    transpose x2, local copies, waits for them, and re-layouts, arrange_rows(): shaped.transpose(0, 2, 3, 1, 4)  26 us
  transfers between devices with their start and end apart: 6, of which 4 were waited for; matrix products, arithmetic and copies ran while one was open for 13% of the time, Pallas kernels for 0%

commit v1 on v0

--- a/solution.py
+++ b/solution.py
@@ -220,7 +220,7 @@
         jnp.bfloat16
     )[None]
     scaled = grad_normed * norm_gain[None, :]
-    inner_sum = lax.psum(jnp.sum(hidden_f * scaled, axis=1), ("exp", "dp"))
+    inner_sum = jnp.sum(lax.all_gather(jnp.sum(hidden_f * scaled, axis=1), ("exp", "dp")), axis=0)
     projection = (inner_sum / model_width)[:, None]
     grad_hidden = (
         out_grad.astype(jnp.float32) + inv_rms * scaled - hidden_f * inv_rms**3 * projection

time: 657 us -> 682 us (1.038)
  blocking collectives: 259 us -> 276 us
  waiting for transfers between devices: 179 us -> 187 us
    reduce_scatter x1, waiting for transfers between devices: 60.3 us -> 81 us  [per_device(): lax.psum_scatter(arrange_sums(full_out, ctx_count, dp_count, exp_count, c...]
    all_gather x0 -> x1, blocking collectives: none -> 17.4 us  [per_device(): lax.all_gather(jnp.sum(hidden_f * scaled, axis=1), ('exp', 'dp'))]
    reduce_scatter x1, waiting for transfers between devices: 81.2 us -> 70.1 us  [per_device(): lax.psum_scatter(arrange_sums(full_back, ctx_count, dp_count, exp_count,...]
    unnamed x55 -> x43, local copies, waits for them, and re-layouts: 19.4 us -> 17.2 us
  transfers between devices with their start and end apart: 6 -> 6, of which waited for: 4 -> 3; matrix products, arithmetic and copies ran while one was open for 13% -> 15% of each run, Pallas kernels for 0% -> 0%
where the time goes in v1:
time: 682 us; the launch traced here: 676 us
  blocking collectives  276 us (40%)
  waiting for transfers between devices  187 us (27%)
  local copies, waits for them, and re-layouts  113 us (17%)
  matrix products  38.9 us (6%)
  other arithmetic  30.4 us (4%)
  starting transfers between devices  15.3 us (2%)
  between operations  14.5 us (2%)
    reduce_scatter x1, waiting for transfers between devices, per_device(): lax.psum_scatter(arrange_sums(full_out, ctx_count, dp_count, exp_count, c...  81 us
    reduce_scatter x1, waiting for transfers between devices, per_device(): lax.psum_scatter(arrange_sums(full_back, ctx_count, dp_count, exp_count,...  70.1 us
    all_gather x2, blocking collectives, entering(): lax.all_gather(a.astype(kind), axis)  48.3 us
    psum x1, blocking collectives, per_device(): grad_probs = lax.psum(probs_part, ('exp', 'dp'))  45.8 us
    psum x1, blocking collectives, per_device(): lax.psum((keys_first + keys_second).astype(jnp.bfloat16), ('exp', 'dp'))  45.7 us
    psum x1, blocking collectives, per_device(): grad_gain = lax.psum(gain_part, 'ctx')  39 us
    all_gather x1, waiting for transfers between devices, per_device(): all_rows = lax.all_gather(got_rows, ('ctx', 'dp'), axis=0, tiled=True)  35.8 us
    transpose x2, local copies, waits for them, and re-layouts, arrange_rows(): shaped.transpose(0, 2, 3, 1, 4)  26 us
  transfers between devices with their start and end apart: 6, of which 3 were waited for; matrix products, arithmetic and copies ran while one was open for 15% of the time, Pallas kernels for 0%

profile of v1, /device:TPU:2, one launch (start us, length us, event | category | flops | bytes accessed | tf_op | source)
XLA Modules:
  0.0 675.5 jit_solution(13509943696238013684)
XLA Ops:
  7.3 0.9 copy.158
  9.5 0.8 copy.161
  10.4 0.9 broadcast_in_dim.74
  11.6 13.2 %scatter_fusion = bf16[8,40,256]{2,1,0:T(8,128)(2,1)S(1)} fusion(bf16[8,40,256]{2,1,0:T(8,128)(2,1)S(1)} %broadcast_in_dim.73.clone.1, s32[256]{0:T(256)S(1)} %bitcast.194, bf16[256,256]{1,0:T(8,128)(2,1)S(1)} %fusion.19), kind=kCustom, calls=%fused_computation.2 | custom fusion | bytes 395264 | tf_op jit(solution)/shard_map/scatter | solution.py:188
  24.9 18.0 %all_to_all.66 = bf16[8,40,1,256]{3,1,2,0:T(8,128)(2,1)S(1)} all-to-all(bf16[8,40,1,256]{3,1,2,0:T(8,128)(2,1)S(1)} %bitcast.201), channel_id=1, replica_groups=mesh['ctx'=16,'exp'=8,'dp'=2] {'exp'}, dimensions={0} | all-to-all | bytes 327680 | tf_op jit(solution)/shard_map/all_to_all | solution.py:189
  44.6 20.7 %all-gather.5 = bf16[16,1,4]{2,1,0:T(2,128)(2,1)S(1)} all-gather(bf16[1,1,4]{2,1,0:T(2,128)(2,1)S(1)} %get-tuple-element.297), channel_id=1, replica_groups=mesh['ctx'=16,'exp'=8,'dp'=2] {'ctx'}, dimensions={0}, use_global_device_ids=true | all-gather | bytes 136 | tf_op jit(solution)/shard_map/all_gather | solution.py:13
  65.4 1.0 copy.152
  67.0 27.6 %all-gather = bf16[64,64,64]{2,1,0:T(8,128)(2,1)} all-gather(bf16[4,64,64]{2,1,0:T(8,128)(2,1)S(1)} %convolution_convert_fusion.4), channel_id=2, replica_groups=mesh['ctx'=16,'exp'=8,'dp'=2] {'ctx'}, dimensions={0}, use_global_device_ids=true | all-gather | bytes 557056 | tf_op jit(solution)/shard_map/all_gather | solution.py:13
  94.8 1.0 while.26
  94.9 0.9 convert_add_fusion.4
  96.7 23.5 %psum.35 = f32[128]{0:T(128)S(1)} all-reduce(f32[128]{0:T(128)S(1)} %get-tuple-element.289), channel_id=1, replica_groups=mesh['ctx'=16,'exp'=8,'dp'=2] {'exp','dp'}, use_global_device_ids=true, to_apply=%region_4.5 | all-reduce | flops 128 | bytes 1024 | tf_op jit(solution)/shard_map/psum | solution.py:153
  121.1 13.2 %scatter_fusion.1 = bf16[8,40,256]{2,1,0:T(8,128)(2,1)S(1)} fusion(bf16[8,40,256]{2,1,0:T(8,128)(2,1)S(1)} %broadcast_in_dim.73.clone, s32[256]{0:T(256)S(1)} %bitcast.195, bf16[256,256]{1,0:T(8,128)(2,1)S(1)} %reshape.275), kind=kCustom, calls=%fused_computation.3 | custom fusion | bytes 395264 | tf_op jit(solution)/shard_map/scatter | solution.py:162
  134.3 12.5 %all_to_all.67 = bf16[8,40,1,256]{3,1,2,0:T(8,128)(2,1)S(1)} all-to-all(bf16[8,40,1,256]{3,1,2,0:T(8,128)(2,1)S(1)} %bitcast.200), channel_id=1, replica_groups=mesh['ctx'=16,'exp'=8,'dp'=2] {'exp'}, dimensions={0} | all-to-all | bytes 327680 | tf_op jit(solution)/shard_map/all_to_all | solution.py:163
  148.1 13.0 %copy.164 = bf16[16,40,8,2,256]{4,3,2,1,0:T(2,128)(2,1)} copy(bf16[16,40,8,2,256]{4,2,1,3,0:T(8,128)(2,1)} %bitcast.204) | data formatting | bytes 10485760 | tf_op jit(solution)/shard_map/transpose | solution.py:105
  161.1 9.6 %reshape.238 = bf16[640,4096]{1,0:T(8,128)(2,1)} reshape(bf16[16,40,8,2,256]{4,3,2,1,0:T(2,128)(2,1)} %copy.164) | data formatting | bytes 10485760 | tf_op jit(solution)/shard_map/reshape | solution.py:105
  170.7 35.8 %all-gather.12.cloned.1.call-done = bf16[32,40,8,1,256]{4,2,3,1,0:T(8,128)(2,1)} async-done(((bf16[1,40,8,1,256]{4,2,3,1,0:T(8,128)(2,1)}), bf16[32,40,8,1,256]{4,2,3,1,0:T(8,128)(2,1)}) %all-gather.12.cloned.1.call-update) | async-done | bytes 5242896 | tf_op jit(solution)/shard_map/all_gather | solution.py:164
  206.6 13.0 %copy.167 = bf16[16,40,8,2,256]{4,3,2,1,0:T(2,128)(2,1)} copy(bf16[16,40,8,2,256]{4,2,1,3,0:T(8,128)(2,1)} %bitcast.205) | data formatting | bytes 10485760 | tf_op jit(solution)/shard_map/transpose | solution.py:105
  219.6 9.6 %reshape.242 = bf16[640,4096]{1,0:T(8,128)(2,1)} reshape(bf16[16,40,8,2,256]{4,3,2,1,0:T(2,128)(2,1)} %copy.167) | data formatting | bytes 10485760 | tf_op jit(solution)/shard_map/reshape | solution.py:105
  229.2 4.2 fusion.10
  233.9 1.5 fusion.5
  235.5 2.4 multiply_convert_fusion
  238.0 1.6 fusion.3
  239.6 3.9 add_convert_fusion
  243.5 9.4 %convert_element_type.165 = bf16[16,40,8,2,256]{4,3,2,1,0:T(2,128)(2,1)} reshape(bf16[640,4096]{1,0:T(8,128)(2,1)} %add_convert_fusion) | data formatting | bytes 10485760 | tf_op jit(solution)/shard_map/convert_element_type | solution.py:201
  252.9 3.4 copy.168
  256.4 4.5 copy.189
  261.4 2.5 convert_bitcast_fusion
  263.9 2.3 copy.176
  266.3 4.6 copy.191
  271.0 5.9 fusion.2
  276.9 5.8 fusion
  282.7 70.1 %reduce-scatter.3.cloned.1.call-done = bf16[40,2048]{1,0:T(8,128)(2,1)} async-done(((bf16[1280,2048]{1,0:T(8,128)(2,1)}), bf16[40,2048]{1,0:T(8,128)(2,1)}) %reduce-scatter.3.cloned.1.call-update) | async-done | bytes 163856 | tf_op jit(solution)/shard_map/reduce_scatter | solution.py:200
  352.8 0.9 copy.190
  354.5 7.2 %all-to-all-start.2 = ((bf16[1,40,8,256]{3,1,0,2:T(8,128)(2,1)}), bf16[1,40,8,256]{3,1,0,2:T(8,128)(2,1)S(1)}, u32[]{:S(2)}, u32[]{:S(2)}) async-start(bf16[1,40,8,256]{3,1,0,2:T(8,128)(2,1)} %copy.169), calls=%async_computation.3 | async-start | bytes 327680 | tf_op jit(solution)/shard_map/all_to_all | solution.py:207
  361.7 5.7 fusion.1
  367.5 81.0 %reduce-scatter.5.cloned.1.call-done = bf16[40,2048]{1,0:T(8,128)(2,1)} async-done(((bf16[1280,2048]{1,0:T(8,128)(2,1)}), bf16[40,2048]{1,0:T(8,128)(2,1)}) %reduce-scatter.5.cloned.1.call-update) | async-done | bytes 163856 | tf_op jit(solution)/shard_map/reduce_scatter | solution.py:173
  448.5 0.9 copy.192
  450.1 7.0 %all-to-all-start.3 = ((bf16[1,40,8,256]{3,1,0,2:T(8,128)(2,1)}), bf16[1,40,8,256]{3,1,0,2:T(8,128)(2,1)S(1)}, u32[]{:S(2)}, u32[]{:S(2)}) async-start(bf16[1,40,8,256]{3,1,0,2:T(8,128)(2,1)} %copy.177), calls=%async_computation.5 | async-start | bytes 327680 | tf_op jit(solution)/shard_map/all_to_all | solution.py:180
  457.1 1.7 gather_fusion
  459.4 17.4 %all-gather.6 = f32[16,1,128]{2,1,0:T(1,128)S(1)} all-gather(f32[1,1,128]{2,1,0:T(1,128)S(1)} %bitcast.228), channel_id=5, replica_groups=mesh['ctx'=16,'exp'=8,'dp'=2] {'exp','dp'}, dimensions={0}, use_global_device_ids=true | all-gather | bytes 8704 | tf_op jit(solution)/shard_map/all_gather | solution.py:223
  478.3 25.5 %all-gather.4 = bf16[64,64,64]{2,1,0:T(8,128)(2,1)} all-gather(bf16[4,64,64]{2,1,0:T(8,128)(2,1)S(1)} %convolution_convert_fusion.3), channel_id=6, replica_groups=mesh['ctx'=16,'exp'=8,'dp'=2] {'ctx'}, dimensions={0}, use_global_device_ids=true | all-gather | bytes 557056 | tf_op jit(solution)/shard_map/all_gather | solution.py:35
  503.8 22.9 %while.27 = (s32[]{:T(128)}, f32[4,64,64]{2,1,0:T(8,128)S(1)}, s32[]{:T(128)}, bf16[16,4]{1,0:T(8,128)(2,1)}, bf16[16,4,64,64]{3,2,1,0:T(8,128)(2,1)}, /*index=5*/s32[]{:T(128)}, s32[]{:T(128)}, s32[]{:T(128)}, s32[]{:T(128)}) while((s32[]{:T(128)}, f32[4,64,64]{2,1,0:T(8,128)S(1)}, s32[]{:T(128)}, bf16[16,4]{1,0:T(8,128)(2,1)}, ...), condition=%wide.region_15.16_spmd, body=%wide.region_14.15_spmd.sunk | while | flops 49162 | bytes 164035 | solution.py:52
  504.5 0.9 convert_add_fusion.5
  506.1 0.9 convert_add_fusion.5
  507.8 0.9 convert_add_fusion.5
  509.4 0.9 convert_add_fusion.5
  511.1 0.9 convert_add_fusion.5
  512.7 0.9 convert_add_fusion.5
  514.3 0.9 convert_add_fusion.5
  516.0 0.9 convert_add_fusion.5
  517.6 0.9 convert_add_fusion.5
  519.3 0.9 convert_add_fusion.5
  520.9 0.9 convert_add_fusion.5
  522.5 0.9 convert_add_fusion.5
  524.2 0.9 convert_add_fusion.5
  525.8 0.9 convert_add_fusion.5
  527.1 1.7 gather_fusion.1
  529.0 45.8 %psum.38 = f32[128,2]{1,0:T(8,128)S(1)} all-reduce(f32[128,2]{1,0:T(8,128)S(1)} %reshape.249), channel_id=1, replica_groups=mesh['ctx'=16,'exp'=8,'dp'=2] {'exp','dp'}, use_global_device_ids=true, to_apply=%region_28.29 | all-reduce | flops 256 | bytes 2048 | tf_op jit(solution)/shard_map/psum | solution.py:187
  575.4 39.0 %psum.39 = f32[256]{0:T(256)} all-reduce(f32[256]{0:T(256)S(1)} %get-tuple-element.263), channel_id=1, replica_groups=mesh['ctx'=16,'exp'=8,'dp'=2] {'ctx'}, use_global_device_ids=true, to_apply=%region_30.31 | all-reduce | flops 256 | bytes 2048 | tf_op jit(solution)/shard_map/psum | solution.py:229
  614.4 1.4 fusion.26
  616.7 1.3 fusion.14
  618.7 45.7 %all-reduce.1 = (bf16[128,64]{0,1:T(8,128)(2,1)S(1)}, bf16[128,64]{0,1:T(8,128)(2,1)S(1)}) all-reduce(bf16[128,64]{0,1:T(8,128)(2,1)S(1)} %fusion.16, bf16[128,64]{0,1:T(8,128)(2,1)S(1)} %fusion.17), channel_id=1, replica_groups=mesh['ctx'=16,'exp'=8,'dp'=2] {'exp','dp'}, use_global_device_ids=true, to_apply=%region_17.18 | all-reduce | flops 16384 | bytes 65536 | tf_op jit(solution)/shard_map/psum | solution.py:236
  665.9 1.1 reduce_window_sum.47
  667.0 1.1 reduce_window_sum.48
  (129 shorter events, 26.4 us)
Async XLA Ops:
  7.2 222.0 %copy-start = (bf16[1,4096,256]{2,1,0:T(8,128)(2,1)S(1)}, bf16[1,4096,256]{2,1,0:T(8,128)(2,1)}, u32[]{:S(2)}) copy-start(bf16[1,4096,256]{2,1,0:T(8,128)(2,1)} %param.26) | copy-start | bytes 6291460
  7.2 59.6 %copy-start.9 = (bf16[128,64]{0,1:T(8,128)(2,1)S(1)}, bf16[128,64]{0,1:T(8,128)(2,1)}, u32[]{:S(2)}) copy-start(bf16[128,64]{0,1:T(8,128)(2,1)} %param.18) | copy-start | bytes 49156
  7.2 87.4 %copy-start.8 = (bf16[128,64]{0,1:T(8,128)(2,1)S(1)}, bf16[128,64]{0,1:T(8,128)(2,1)}, u32[]{:S(2)}) copy-start(bf16[128,64]{0,1:T(8,128)(2,1)} %param.19) | copy-start | bytes 49156
  7.2 89.4 %copy-start.11 = (bf16[128,256]{1,0:T(8,128)(2,1)S(1)}, bf16[128,256]{1,0:T(8,128)(2,1)}, u32[]{:S(2)}) copy-start(bf16[128,256]{1,0:T(8,128)(2,1)} %param.16) | copy-start | bytes 196612
  7.2 113.6 %copy-start.12 = (f32[256]{0:T(256)S(1)}, f32[256]{0:T(256)}, u32[]{:S(2)}) copy-start(f32[256]{0:T(256)} %param.23) | copy-start | bytes 3076
  7.2 140.9 %all-gather.10.cloned.1.call-start = ((), (), s32[]{:S(2)}) async-start(), calls=%async_computation.8 | async-start | bytes 5406720 | tf_op jit(solution)/shard_map/all_gather | solution.py:190
  43.6 162.9 %all-gather.12.cloned.1.call-start = ((), (), s32[]{:S(2)}) async-start(), calls=%async_computation.9 | async-start | bytes 5406720 | tf_op jit(solution)/shard_map/all_gather | solution.py:164
  66.4 67.9 %copy-start.14 = (f32[4,128]{1,0:T(4,128)}, f32[4,128]{1,0:T(4,128)S(1)}, u32[]{:S(2)}) copy-start(f32[4,128]{1,0:T(4,128)S(1)} %copy.150) | copy-start | bytes 6148
  94.8 66.3 %copy-start.10 = (f32[128,128]{1,0:T(8,128)}, f32[128,128]{1,0:T(8,128)S(1)}, u32[]{:S(2)}) copy-start(f32[128,128]{1,0:T(8,128)S(1)} %fusion.65) | copy-start | bytes 196612
  95.8 38.5 %copy-start.13 = (bf16[16,4]{1,0:T(8,128)(2,1)}, bf16[16,4]{1,0:T(8,128)(2,1)S(1)}, u32[]{:S(2)}) copy-start(bf16[16,4]{1,0:T(8,128)(2,1)S(1)} %get-tuple-element.435) | copy-start | bytes 388
  147.5 205.4 %reduce-scatter.3.cloned.1.call-start = ((), (), s32[]{:S(2)}) async-start(), calls=%async_computation.6 | async-start | bytes 5406720 | tf_op jit(solution)/shard_map/reduce_scatter | solution.py:200
  229.2 4.2 copy-start.1
  229.2 4.7 copy-start.2
  233.9 1.6 copy-start.3
  238.0 1.6 copy-start.4
  238.0 1.6 copy-start.6
  260.9 187.6 %reduce-scatter.5.cloned.1.call-start = ((), (), s32[]{:S(2)}) async-start(), calls=%async_computation.7 | async-start | bytes 5406720 | tf_op jit(solution)/shard_map/reduce_scatter | solution.py:173
  270.9 5.9 copy-start.5
  354.5 95.7 %all-to-all-start.2 = ((bf16[1,40,8,256]{3,1,0,2:T(8,128)(2,1)}), bf16[1,40,8,256]{3,1,0,2:T(8,128)(2,1)S(1)}, u32[]{:S(2)}, u32[]{:S(2)}) async-start(bf16[1,40,8,256]{3,1,0,2:T(8,128)(2,1)} %copy.169), calls=%async_computation.3 | async-start | bytes 327680 | tf_op jit(solution)/shard_map/all_to_all | solution.py:207
  361.7 115.1 %copy-start.7 = (bf16[128,256]{1,0:T(8,128)(2,1)S(1)}, bf16[128,256]{1,0:T(8,128)(2,1)}, u32[]{:S(2)}) copy-start(bf16[128,256]{1,0:T(8,128)(2,1)} %param.27) | copy-start | bytes 196612
  361.7 115.1 %copy-start.15 = (f32[128]{0:T(128)S(1)}, f32[128]{0:T(128)}, u32[]{:S(2)}) copy-start(f32[128]{0:T(128)} %get-tuple-element.298) | copy-start | bytes 1540
  450.1 76.9 %all-to-all-start.3 = ((bf16[1,40,8,256]{3,1,0,2:T(8,128)(2,1)}), bf16[1,40,8,256]{3,1,0,2:T(8,128)(2,1)S(1)}, u32[]{:S(2)}, u32[]{:S(2)}) async-start(bf16[1,40,8,256]{3,1,0,2:T(8,128)(2,1)} %copy.177), calls=%async_computation.5 | async-start | bytes 327680 | tf_op jit(solution)/shard_map/all_to_all | solution.py:180
Sparse Core Ops, SparseCore 0:
  43.7 49.1 all-gather.9
  147.6 58.8 all-gather.11
  261.0 91.7 reduce-scatter.2
  356.7 91.7 reduce-scatter.4
